TPU v7x, 32 devices: a whole 2x2x4 slice. The times are simulated.
32 devices in a mesh: dp: 16 (over z, y, core), fsdp: 2 (over x).
Axes of the slice: x: 2, y: 2, z: 4, core: 2. Of those that a mesh axis runs over, the one named last changes fastest.
Arguments:
- tokens: bfloat16 [32768, 768], P(('dp', 'fsdp')), may hold values from -6 to 6
- segment_ids: int32 [32768], P(('dp', 'fsdp')), may hold values from 0 to 255, never falling along the last dimension, each value on 1 to 384 neighbouring positions
- cotangent: bfloat16 [32768, 768], P(('dp', 'fsdp')), may hold values from -6 to 6
- norm1_gain: float32 [768], P('fsdp'), may hold values from 0.5 to 1.5
- norm1_shift: float32 [768], P('fsdp'), may hold values from -1.75 to 1.75
- qkv_weight: float32 [768, 2304], P('fsdp'), may hold values from -0.21875 to 0.21875
- query_bias: float32 [768], P('fsdp'), may hold values from -3 to 3
- value_bias: float32 [768], P('fsdp'), may hold values from -3 to 3
- out_weight: float32 [768, 768], P('fsdp'), may hold values from -1.75 to 1.75
- out_bias: float32 [768], P('fsdp'), may hold values from -1.75 to 1.75
- norm2_gain: float32 [768], P('fsdp'), may hold values from 0.5 to 1.5
- norm2_shift: float32 [768], P('fsdp'), may hold values from -1.75 to 1.75
- up_weight: float32 [768, 3072], P('fsdp'), may hold values from -0.21875 to 0.21875
- up_bias: float32 [3072], P('fsdp'), may hold values from -3 to 3
- down_weight: float32 [3072, 768], P('fsdp'), may hold values from -0.109375 to 0.109375
- down_bias: float32 [768], P('fsdp'), may hold values from -1.75 to 1.75
Outputs:
- output: bfloat16 [32768, 768], P(('dp', 'fsdp'))
- input_grad: bfloat16 [32768, 768], P(('dp', 'fsdp'))
- norm1_gain_grad: float32 [768], P('fsdp')
- norm1_shift_grad: float32 [768], P('fsdp')
- qkv_weight_grad: float32 [768, 2304], P('fsdp')
- query_bias_grad: float32 [768], P('fsdp')
- value_bias_grad: float32 [768], P('fsdp')
- out_weight_grad: float32 [768, 768], P('fsdp')
- out_bias_grad: float32 [768], P('fsdp')
- norm2_gain_grad: float32 [768], P('fsdp')
- norm2_shift_grad: float32 [768], P('fsdp')
- up_weight_grad: float32 [768, 3072], P('fsdp')
- up_bias_grad: float32 [3072], P('fsdp')
- down_weight_grad: float32 [3072, 768], P('fsdp')
- down_bias_grad: float32 [768], P('fsdp')
Inputs may be any that keep to these rules, and one draw needn't show every extreme that they name: segment_ids never fall along the rows; each id covers 1 to 384 consecutive rows and some id covers exactly 384.
All inputs are finite; a program needn't handle non-finite values.
Results may differ from a plain program's by a relative error of at most 0.019.
Values may be sent and summed in bfloat16 or wider, within the bound.
A program may use at most 192 MiB of HBM per device.

v0:
```python
import jax
import jax.numpy as jnp
from jax import lax
from jax.sharding import PartitionSpec as P

HEADS = 12
SEQ = 512
EPSILON = 1e-06
LARGE_NEG = -1000000000.0


def layer_norm(inputs, gain_vec, shift_vec):
    centre = inputs - jnp.mean(inputs, -1, keepdims=True)
    spread = jnp.mean(centre * centre, -1, keepdims=True)
    return centre * lax.rsqrt(spread + EPSILON) * gain_vec + shift_vec


def gelu_exact(inputs):
    return jax.nn.gelu(inputs, approximate=False)


def matmul(left, right):
    return jnp.dot(left, right, preferred_element_type=jnp.float32)


def outer_sum(left, right):
    return jnp.einsum("ta,tb->ab", left, right, preferred_element_type=jnp.float32)


def back_mul(left, right):
    return jnp.einsum("tb,ab->ta", left, right, preferred_element_type=jnp.float32)


def column_sum(values_b):
    return jnp.sum(values_b.astype(jnp.float32), 0)


def scores_of(queries, key_rows, seg_block, scaling):
    raw_scores = jnp.einsum("qhd,khd->hqk", queries, key_rows, preferred_element_type=jnp.float32)
    allowed = seg_block[:, None] == seg_block[None, :]
    return jnp.where(allowed[None], raw_scores * scaling, LARGE_NEG)


def body(
    tokens,
    segment_ids,
    cotangent,
    norm1_gain,
    norm1_shift,
    qkv_weight,
    query_bias,
    value_bias,
    out_weight,
    out_bias,
    norm2_gain,
    norm2_shift,
    up_weight,
    up_bias,
    down_weight,
    down_bias,
):
    masters = [
        norm1_gain,
        norm1_shift,
        qkv_weight,
        query_bias,
        value_bias,
        out_weight,
        out_bias,
        norm2_gain,
        norm2_shift,
        up_weight,
        up_bias,
        down_weight,
        down_bias,
    ]
    rounded_params = [master.astype(jnp.bfloat16) for master in masters]
    fwd_params = (
        lax.all_gather(rounded_params[0], "fsdp", axis=0, tiled=True),
        lax.all_gather(rounded_params[1], "fsdp", axis=0, tiled=True),
        lax.all_gather(rounded_params[2], "fsdp", axis=0, tiled=True),
        lax.all_gather(rounded_params[3], "fsdp", axis=0, tiled=True),
        lax.all_gather(rounded_params[4], "fsdp", axis=0, tiled=True),
        lax.all_gather(rounded_params[5], "fsdp", axis=0, tiled=True),
        lax.all_gather(rounded_params[6], "fsdp", axis=0, tiled=True),
        lax.all_gather(rounded_params[7], "fsdp", axis=0, tiled=True),
        lax.all_gather(rounded_params[8], "fsdp", axis=0, tiled=True),
        lax.all_gather(rounded_params[9], "fsdp", axis=0, tiled=True),
        lax.all_gather(rounded_params[10], "fsdp", axis=0, tiled=True),
        lax.all_gather(rounded_params[11], "fsdp", axis=0, tiled=True),
        lax.all_gather(rounded_params[12], "fsdp", axis=0, tiled=True),
    )
    gain_one = fwd_params[0].astype(jnp.float32)
    shift_one = fwd_params[1].astype(jnp.float32)
    q_bias = fwd_params[3].astype(jnp.float32)
    v_bias = fwd_params[4].astype(jnp.float32)
    o_bias = fwd_params[6].astype(jnp.float32)
    gain_two = fwd_params[7].astype(jnp.float32)
    shift_two = fwd_params[8].astype(jnp.float32)
    u_bias = fwd_params[10].astype(jnp.float32)
    d_bias = fwd_params[12].astype(jnp.float32)
    rows_here = tokens.shape[0]
    width = tokens.shape[1]
    seq_here = rows_here // SEQ
    head_dim = width // HEADS
    scaling = head_dim ** (-0.5)
    seg_blocks = segment_ids.reshape(seq_here, SEQ)

    def attend_forward(block):
        queries, key_rows, value_rows, seg_block = block
        scores = scores_of(queries, key_rows, seg_block, scaling)
        row_max = jnp.max(scores, -1, keepdims=True)
        row_total = jnp.sum(jnp.exp(scores - row_max), -1, keepdims=True)
        log_total = row_max + jnp.log(row_total)
        attn_b = jnp.exp(scores - log_total).astype(jnp.bfloat16)
        att_out = jnp.einsum("hqk,khd->qhd", attn_b, value_rows, preferred_element_type=jnp.float32)
        return (att_out.astype(jnp.bfloat16), log_total)

    def attend_backward(block):
        queries, key_rows, value_rows, seg_block, log_total, grad_att = block
        scores = scores_of(queries, key_rows, seg_block, scaling)
        attn_f = jnp.exp(scores - log_total)
        attn_b = attn_f.astype(jnp.bfloat16)
        grad_values = jnp.einsum(
            "hqk,qhd->khd", attn_b, grad_att, preferred_element_type=jnp.float32
        )
        grad_attn = jnp.einsum(
            "qhd,khd->hqk", grad_att, value_rows, preferred_element_type=jnp.float32
        )
        row_dot = jnp.sum(grad_attn * attn_f, -1, keepdims=True)
        grad_scores = (attn_f * (grad_attn - row_dot)).astype(jnp.bfloat16)
        grad_queries = (
            jnp.einsum("hqk,khd->qhd", grad_scores, key_rows, preferred_element_type=jnp.float32)
            * scaling
        )
        grad_keys = (
            jnp.einsum("hqk,qhd->khd", grad_scores, queries, preferred_element_type=jnp.float32)
            * scaling
        )
        return (
            grad_queries.astype(jnp.bfloat16),
            grad_keys.astype(jnp.bfloat16),
            grad_values.astype(jnp.bfloat16),
        )

    inputs = tokens.astype(jnp.float32)
    normed_one, norm_one_pull = jax.vjp(layer_norm, inputs, gain_one, shift_one)
    act_one = normed_one.astype(jnp.bfloat16)
    linear = matmul(act_one, fwd_params[2]) + jnp.concatenate(
        [q_bias, jnp.zeros_like(q_bias), v_bias]
    )
    linear_b = linear.astype(jnp.bfloat16)
    queries = linear_b[:, :width].reshape(seq_here, SEQ, HEADS, head_dim)
    key_rows = linear_b[:, width : 2 * width].reshape(seq_here, SEQ, HEADS, head_dim)
    value_rows = linear_b[:, 2 * width :].reshape(seq_here, SEQ, HEADS, head_dim)
    attended, log_totals = lax.map(attend_forward, (queries, key_rows, value_rows, seg_blocks))
    attended = attended.reshape(rows_here, width)
    branch = matmul(attended, fwd_params[5]) + o_bias
    middle = inputs + branch
    normed_two, norm_two_pull = jax.vjp(layer_norm, middle, gain_two, shift_two)
    act_two = normed_two.astype(jnp.bfloat16)
    hidden_pre = matmul(act_two, fwd_params[9]) + u_bias
    gelu_out, gelu_pull = jax.vjp(gelu_exact, hidden_pre)
    hidden_b = gelu_out.astype(jnp.bfloat16)
    mlp_out = matmul(hidden_b, fwd_params[11]) + d_bias
    output = (middle + mlp_out).astype(jnp.bfloat16)
    back_params = (
        lax.all_gather(rounded_params[0], "fsdp", axis=0, tiled=True),
        lax.all_gather(rounded_params[1], "fsdp", axis=0, tiled=True),
        lax.all_gather(rounded_params[2], "fsdp", axis=0, tiled=True),
        lax.all_gather(rounded_params[3], "fsdp", axis=0, tiled=True),
        lax.all_gather(rounded_params[4], "fsdp", axis=0, tiled=True),
        lax.all_gather(rounded_params[5], "fsdp", axis=0, tiled=True),
        lax.all_gather(rounded_params[6], "fsdp", axis=0, tiled=True),
        lax.all_gather(rounded_params[7], "fsdp", axis=0, tiled=True),
        lax.all_gather(rounded_params[8], "fsdp", axis=0, tiled=True),
        lax.all_gather(rounded_params[9], "fsdp", axis=0, tiled=True),
        lax.all_gather(rounded_params[10], "fsdp", axis=0, tiled=True),
        lax.all_gather(rounded_params[11], "fsdp", axis=0, tiled=True),
        lax.all_gather(rounded_params[12], "fsdp", axis=0, tiled=True),
    )
    grad_out = cotangent.astype(jnp.float32)
    grad_wdown = outer_sum(hidden_b, cotangent)
    grad_dbias = jnp.sum(grad_out, 0)
    grad_hidden = back_mul(cotangent, back_params[11])
    grad_pre_b = gelu_pull(grad_hidden)[0].astype(jnp.bfloat16)
    grad_wup = outer_sum(act_two, grad_pre_b)
    grad_ubias = column_sum(grad_pre_b)
    grad_act_two = back_mul(grad_pre_b, back_params[9])
    grad_mid_norm, grad_gain_two, grad_shift_two = norm_two_pull(grad_act_two)
    grad_middle = grad_out + grad_mid_norm
    mlp_shards = (
        lax.psum_scatter(
            grad_wup.astype(jnp.bfloat16), "fsdp", scatter_dimension=0, tiled=True
        ).astype(jnp.float32),
        lax.psum_scatter(
            grad_ubias.astype(jnp.bfloat16), "fsdp", scatter_dimension=0, tiled=True
        ).astype(jnp.float32),
        lax.psum_scatter(
            grad_wdown.astype(jnp.bfloat16), "fsdp", scatter_dimension=0, tiled=True
        ).astype(jnp.float32),
        lax.psum_scatter(
            grad_dbias.astype(jnp.bfloat16), "fsdp", scatter_dimension=0, tiled=True
        ).astype(jnp.float32),
        lax.psum_scatter(
            grad_gain_two.astype(jnp.bfloat16), "fsdp", scatter_dimension=0, tiled=True
        ).astype(jnp.float32),
        lax.psum_scatter(
            grad_shift_two.astype(jnp.bfloat16), "fsdp", scatter_dimension=0, tiled=True
        ).astype(jnp.float32),
    )
    mlp_grads = (
        lax.psum(mlp_shards[0].astype(jnp.bfloat16), "dp").astype(jnp.float32),
        lax.psum(mlp_shards[1].astype(jnp.bfloat16), "dp").astype(jnp.float32),
        lax.psum(mlp_shards[2].astype(jnp.bfloat16), "dp").astype(jnp.float32),
        lax.psum(mlp_shards[3].astype(jnp.bfloat16), "dp").astype(jnp.float32),
        lax.psum(mlp_shards[4].astype(jnp.bfloat16), "dp").astype(jnp.float32),
        lax.psum(mlp_shards[5].astype(jnp.bfloat16), "dp").astype(jnp.float32),
    )
    grad_branch_b = grad_middle.astype(jnp.bfloat16)
    grad_wout = outer_sum(attended, grad_branch_b)
    grad_obias = column_sum(grad_branch_b)
    grad_att_b = back_mul(grad_branch_b, back_params[5]).astype(jnp.bfloat16)
    grad_att_b = grad_att_b.reshape(seq_here, SEQ, HEADS, head_dim)
    grad_q_b, grad_k_b, grad_v_b = lax.map(
        attend_backward, (queries, key_rows, value_rows, seg_blocks, log_totals, grad_att_b)
    )
    grad_q_b = grad_q_b.reshape(rows_here, width)
    grad_k_b = grad_k_b.reshape(rows_here, width)
    grad_v_b = grad_v_b.reshape(rows_here, width)
    grad_linear_b = jnp.concatenate([grad_q_b, grad_k_b, grad_v_b], 1)
    grad_wqkv = outer_sum(act_one, grad_linear_b)
    grad_qbias = column_sum(grad_q_b)
    grad_vbias = column_sum(grad_v_b)
    grad_act_one = back_mul(grad_linear_b, back_params[2])
    grad_in_norm, grad_gain_one, grad_shift_one = norm_one_pull(grad_act_one)
    input_grad = (grad_middle + grad_in_norm).astype(jnp.bfloat16)
    attn_shards = (
        lax.psum_scatter(
            grad_gain_one.astype(jnp.bfloat16), "fsdp", scatter_dimension=0, tiled=True
        ).astype(jnp.float32),
        lax.psum_scatter(
            grad_shift_one.astype(jnp.bfloat16), "fsdp", scatter_dimension=0, tiled=True
        ).astype(jnp.float32),
        lax.psum_scatter(
            grad_wqkv.astype(jnp.bfloat16), "fsdp", scatter_dimension=0, tiled=True
        ).astype(jnp.float32),
        lax.psum_scatter(
            grad_qbias.astype(jnp.bfloat16), "fsdp", scatter_dimension=0, tiled=True
        ).astype(jnp.float32),
        lax.psum_scatter(
            grad_vbias.astype(jnp.bfloat16), "fsdp", scatter_dimension=0, tiled=True
        ).astype(jnp.float32),
        lax.psum_scatter(
            grad_wout.astype(jnp.bfloat16), "fsdp", scatter_dimension=0, tiled=True
        ).astype(jnp.float32),
        lax.psum_scatter(
            grad_obias.astype(jnp.bfloat16), "fsdp", scatter_dimension=0, tiled=True
        ).astype(jnp.float32),
    )
    attn_grads = (
        lax.psum(attn_shards[0].astype(jnp.bfloat16), "dp").astype(jnp.float32),
        lax.psum(attn_shards[1].astype(jnp.bfloat16), "dp").astype(jnp.float32),
        lax.psum(attn_shards[2].astype(jnp.bfloat16), "dp").astype(jnp.float32),
        lax.psum(attn_shards[3].astype(jnp.bfloat16), "dp").astype(jnp.float32),
        lax.psum(attn_shards[4].astype(jnp.bfloat16), "dp").astype(jnp.float32),
        lax.psum(attn_shards[5].astype(jnp.bfloat16), "dp").astype(jnp.float32),
        lax.psum(attn_shards[6].astype(jnp.bfloat16), "dp").astype(jnp.float32),
    )
    return (
        output,
        input_grad,
        attn_grads[0],
        attn_grads[1],
        attn_grads[2],
        attn_grads[3],
        attn_grads[4],
        attn_grads[5],
        attn_grads[6],
        mlp_grads[4],
        mlp_grads[5],
        mlp_grads[0],
        mlp_grads[1],
        mlp_grads[2],
        mlp_grads[3],
    )


def solution(mesh):
    placed = (
        P(("dp", "fsdp"), None),
        P(("dp", "fsdp")),
        P(("dp", "fsdp"), None),
        P("fsdp"),
        P("fsdp"),
        P("fsdp", None),
        P("fsdp"),
        P("fsdp"),
        P("fsdp", None),
        P("fsdp"),
        P("fsdp"),
        P("fsdp"),
        P("fsdp", None),
        P("fsdp"),
        P("fsdp", None),
        P("fsdp"),
    )
    return jax.shard_map(
        body,
        mesh=mesh,
        in_specs=placed,
        out_specs=(
            P(("dp", "fsdp"), None),
            P(("dp", "fsdp"), None),
            P("fsdp"),
            P("fsdp"),
            P("fsdp", None),
            P("fsdp"),
            P("fsdp"),
            P("fsdp", None),
            P("fsdp"),
            P("fsdp"),
            P("fsdp"),
            P("fsdp", None),
            P("fsdp"),
            P("fsdp", None),
            P("fsdp"),
        ),
        check_vma=False,
    )
```

profile of v0, /device:TPU:0, one launch (start us, length us, event | category | flops | bytes accessed | tf_op | source)
XLA Modules:
  0.0 684.2 jit_solution(3355608891467746422)
XLA Ops:
  63.3 6.4 add_convert_fusion.1
  96.9 20.6 %while.26 = (s32[]{:T(128)}, bf16[2,512,12,64]{1,3,2,0:T(8,128)(2,1)}, f32[2,12,512,1]{2,1,3,0:T(8,128)S(1)}, bf16[2,512,12,64]{1,3,2,0:T(8,128)(2,1)}, s32[2,51...) while((s32[]{:T(128)}, ...), condition=%wide.region_5.6_spmd, body=%wide.region_2.5_spmd.sunk | while | flops 840558592 | bytes 42180708 | solution.py:156
  127.6 25.5 %all-gather.18.cloned.1.call-done = bf16[768,3072]{1,0:T(8,128)(2,1)} async-done(((bf16[384,3072]{1,0:T(8,128)(2,1)}), bf16[768,3072]{1,0:T(8,128)(2,1)}) %all-gather.18.cloned.1.call-update) | async-done | bytes 4718608 | tf_op jit(solution)/shard_map/all_gather | solution.py:88
  153.0 37.7 %multiply_convert_fusion.3 = (bf16[1024,3072]{1,0:T(8,128)(2,1)}, f32[1024,3072]{1,0:T(8,128)}, f32[1024,3072]{1,0:T(8,128)}) fusion(f32[3072]{0:T(1024)S(1)} %bitcast.168, bf16[768,3072]{1,0:T(8,128)(2,1)} %all-gather.18.cloned.1.call-done, f32[1024,768]{0,1:T(8,128)S(1)} %get-tuple-element.284, f32[768]{0:T(1024)S(1)} %reshape.249, ...), kind=kOutput, calls=%fused_computation.68 | convolution fusion | flops 5043388416 | bytes 39348224 | tf_op jit(solution)/shard_map/dot_general | solution.py:23
  190.8 26.9 %all-gather.20.cloned.1.call-done = bf16[3072,768]{1,0:T(8,128)(2,1)} async-done(((bf16[1536,768]{1,0:T(8,128)(2,1)}), bf16[3072,768]{1,0:T(8,128)(2,1)}) %all-gather.20.cloned.1.call-update) | async-done | bytes 4718608 | tf_op jit(solution)/shard_map/all_gather | solution.py:90
  217.7 18.9 %fusion.89 = (bf16[3072]{0:T(1024)(128)(2,1)}, bf16[1024,3072]{1,0:T(8,128)(2,1)}) fusion(f32[1024,3072]{1,0:T(8,128)} %get-tuple-element.275, bf16[1024,768]{1,0:T(8,128)(2,1)} %param.22, bf16[3072,768]{1,0:T(8,128)(2,1)} %all-gather.20.cloned.1.call-done, f32[1024,3072]{1,0:T(8,128)} %get-tuple-element.285, f32[3072]{0:T(1024)S(1)} %bitcast.169), kind=kOutput, calls=%fused_computation.142 | convolution fusion | flops 4882166784 | bytes 37767168 | tf_op jit(solution)/shard_map/tb,ab->ta/dot_general | solution.py:31
  236.6 10.3 %fusion.88 = (bf16[768]{0:T(1024)(128)(2,1)}, f32[1024,768]{1,0:T(8,128)}) fusion(bf16[1024,3072]{1,0:T(8,128)(2,1)} %get-tuple-element.291, bf16[768,3072]{1,0:T(8,128)(2,1)} %all-gather.18.cloned.1.call-done), kind=kOutput, calls=%fused_computation.141 | convolution fusion | flops 4832623616 | bytes 14157312 | tf_op jit(solution)/shard_map/tb,ab->ta/dot_general | solution.py:31
  270.5 49.0 %while.27 = (s32[]{:T(128)}, bf16[2,512,12,64]{1,3,2,0:T(8,128)(2,1)}, bf16[2,512,12,64]{1,3,2,0:T(8,128)(2,1)}, bf16[2,512,12,64]{1,3,2,0:T(8,128)(2,1)}, bf16[...) while((s32[]{:T(128)}, ...), condition=%wide.region_12.13_spmd, body=%wide.region_10.12_spmd.sunk | while | flops 2062673920 | bytes 141233456 | solution.py:225
  276.6 6.9 %multiply_reduce_fusion.5 = (f32[12,512]{1,0:T(8,128)S(1)}, f32[12,512,512]{1,2,0:T(8,128)}) fusion(f32[12,512,512]{1,2,0:T(8,128)S(1)} %fusion.138, f32[12,512]{1,0:T(8,128)S(1)} %dynamic-slice_bitcast_fusion.2, pred[512,512]{0,1:T(8,128)(4,1)S(1)} %broadcast_compare_fusion.5, bf16[2,512,12,64]{1,3,2,0:T(8,128)(2,1)S(1)} %copy-done.10, ...), kind=kOutput, calls=%fused_computation.25.clone.1 | convolution fusion | flops 418375680 | bytes 27059200 | tf_op jit(solution)/shard_map/while/body/eval_jaxpr/qhd,khd->hqk/dot_general | solution.py:127
  283.5 7.1 %multiply_convert_fusion.5 = bf16[12,512,512]{1,2,0:T(8,128)(2,1)S(1)} fusion(f32[12,512,512]{1,2,0:T(8,128)} %get-tuple-element.406, f32[12,512,512]{1,2,0:T(8,128)S(1)} %fusion.138, f32[12,512]{1,0:T(8,128)S(1)} %get-tuple-element.407, f32[12,512]{1,0:T(8,128)S(1)} %dynamic-slice_bitcast_fusion.2, pred[512,512]{0,1:T(8,128)(4,1)S(1)} %broadcast_compare_fusion.5), kind=kLoop, calls=%fused_computation.24.clone.1 | loop fusion | flops 18874368 | bytes 31768576 | tf_op jit(solution)/shard_map/while/body/eval_jaxpr/convert_element_type | solution.py:131
  301.0 6.9 %multiply_reduce_fusion.5 = (f32[12,512]{1,0:T(8,128)S(1)}, f32[12,512,512]{1,2,0:T(8,128)}) fusion(f32[12,512,512]{1,2,0:T(8,128)S(1)} %fusion.138, f32[12,512]{1,0:T(8,128)S(1)} %dynamic-slice_bitcast_fusion.2, pred[512,512]{0,1:T(8,128)(4,1)S(1)} %broadcast_compare_fusion.5, bf16[2,512,12,64]{1,3,2,0:T(8,128)(2,1)S(1)} %copy-done.10, ...), kind=kOutput, calls=%fused_computation.25.clone.1 | convolution fusion | flops 418375680 | bytes 27059200 | tf_op jit(solution)/shard_map/while/body/eval_jaxpr/qhd,khd->hqk/dot_general | solution.py:127
  307.9 7.1 %multiply_convert_fusion.5 = bf16[12,512,512]{1,2,0:T(8,128)(2,1)S(1)} fusion(f32[12,512,512]{1,2,0:T(8,128)} %get-tuple-element.406, f32[12,512,512]{1,2,0:T(8,128)S(1)} %fusion.138, f32[12,512]{1,0:T(8,128)S(1)} %get-tuple-element.407, f32[12,512]{1,0:T(8,128)S(1)} %dynamic-slice_bitcast_fusion.2, pred[512,512]{0,1:T(8,128)(4,1)S(1)} %broadcast_compare_fusion.5), kind=kLoop, calls=%fused_computation.24.clone.1 | loop fusion | flops 18874368 | bytes 31768576 | tf_op jit(solution)/shard_map/while/body/eval_jaxpr/convert_element_type | solution.py:131
  331.2 5.7 convolution_convert_fusion.2
  337.0 9.1 %convolution_convert_fusion = bf16[3072,768]{1,0:T(8,128)(2,1)} fusion(bf16[1024,3072]{1,0:T(8,128)(2,1)} %get-tuple-element.274, bf16[1024,768]{1,0:T(8,128)(2,1)} %param.22), kind=kOutput, calls=%fused_computation.83 | convolution fusion | flops 4834197504 | bytes 12582912 | tf_op jit(solution)/shard_map/ta,tb->ab/dot_general | solution.py:27
  346.8 9.9 %convolution_convert_fusion.1 = bf16[768,3072]{1,0:T(8,128)(2,1)} fusion(bf16[1024,3072]{1,0:T(8,128)(2,1)} %get-tuple-element.291, f32[1024,768]{0,1:T(8,128)} %copy-done.7, f32[768]{0:T(1024)S(1)} %copy-done.51, f32[768]{0:T(1024)S(1)} %copy-done.43, f32[1024]{0:T(1024)S(1)} %copy-done.45, f32[1024]{0:T(1024)S(1)} %copy-done.35), kind=kOutput, calls=%fused_computation.84 | convolution fusion | flops 4838129664 | bytes 14170112 | tf_op jit(solution)/shard_map/ta,tb->ab/dot_general | solution.py:27
  365.4 19.4 %reduce-scatter.5.cloned.1.call-done = bf16[384,2304]{1,0:T(8,128)(2,1)} async-done(((bf16[768,2304]{1,0:T(8,128)(2,1)}), bf16[384,2304]{1,0:T(8,128)(2,1)}) %reduce-scatter.5.cloned.1.call-update) | async-done | bytes 1769488 | tf_op jit(solution)/shard_map/reduce_scatter | solution.py:245
  384.8 62.3 %reduce-scatter.11.cloned.1.call-done = bf16[1536,768]{1,0:T(8,128)(2,1)} async-done(((bf16[3072,768]{1,0:T(8,128)(2,1)}), bf16[1536,768]{1,0:T(8,128)(2,1)}) %reduce-scatter.11.cloned.1.call-update) | async-done | bytes 2359312 | tf_op jit(solution)/shard_map/reduce_scatter | solution.py:199
  447.1 63.0 %reduce-scatter.9.cloned.1.call-done = bf16[384,3072]{1,0:T(8,128)(2,1)} async-done(((bf16[768,3072]{1,0:T(8,128)(2,1)}), bf16[384,3072]{1,0:T(8,128)(2,1)}) %reduce-scatter.9.cloned.1.call-update) | async-done | bytes 2359312 | tf_op jit(solution)/shard_map/reduce_scatter | solution.py:193
  510.2 10.0 %add_convert_fusion.3 = bf16[1024,768]{0,1:T(8,128)(2,1)} fusion(f32[1024,768]{0,1:T(8,128)} %copy-done.7, bf16[1024,3072]{1,0:T(8,128)(2,1)} %get-tuple-element.274, bf16[3072,768]{1,0:T(8,128)(2,1)} %all-gather.20.cloned.1.call-done, f32[768]{0:T(1024)S(1)} %reshape.251), kind=kOutput, calls=%fused_computation.106 | convolution fusion | flops 4834197504 | bytes 15731712 | tf_op jit(solution)/shard_map/dot_general | solution.py:23
  524.9 9.1 %fusion.87 = (bf16[768]{0:T(1024)(128)(2,1)S(1)}, f32[1024,768]{1,0:T(8,128)}) fusion(bf16[1024,2304]{0,1:T(8,128)(2,1)} %copy-done.25, bf16[768,2304]{1,0:T(8,128)(2,1)} %all-gather.14.cloned.1.call-done), kind=kOutput, calls=%fused_computation.140 | convolution fusion | flops 3624664320 | bytes 11404800 | tf_op jit(solution)/shard_map/tb,ab->ta/dot_general | solution.py:31
  541.9 7.4 %all-reduce.11 = (bf16[768]{0:T(1024)(128)(2,1)S(1)}, bf16[768]{0:T(1024)(128)(2,1)S(1)}, bf16[768]{0:T(1024)(128)(2,1)S(1)}, bf16[768]{0:T(1024)(128)(2,1)S(1)}...) all-reduce(bf16[768]{0:T(1024)(128)(2,1)S(1)} %get-tuple-element.21, ...), channel_id=2, replica_groups=mesh['dp'=16,'fsdp'=2] {'fsdp'}, use_global_device_ids=true, to_apply=%region_16.17.clone | all-reduce | flops 9216 | bytes 36864
  550.0 61.8 %all-reduce.9 = (bf16[384]{0:T(512)(128)(2,1)S(1)}, bf16[384]{0:T(512)(128)(2,1)S(1)}, bf16[384]{0:T(512)(128)(2,1)S(1)}, bf16[384]{0:T(512)(128)(2,1)S(1)}, bf1...) all-reduce(bf16[384]{0:T(512)(128)(2,1)S(1)} %dynamic-slice.1, ...), channel_id=1, replica_groups=mesh['dp'=16,'fsdp'=2] {'dp'}, use_global_device_ids=true, to_apply=%region_17.18 | all-reduce | flops 4608 | bytes 18432 | tf_op jit(solution)/shard_map/psum | solution.py:262
  616.5 6.2 add_convert_fusion.2
  625.9 40.3 %all-reduce.14.cloned.1.call-done = (bf16[384,2304]{1,0:T(8,128)(2,1)}, bf16[384,768]{1,0:T(8,128)(2,1)}, bf16[384,3072]{1,0:T(8,128)(2,1)}, bf16[1536,768]{1,0:T(8,128)(2,1)}) async-done(((bf16[384,2304]{1,0:T(8,128)(2,1)}, bf16[384,768]{1,0:T(8,128)(2,1)}, bf16[384,3072]{1,0:T(8,128)(2,1)}, bf16[1536,768]{1,0:T(8,128)(2,1)}), (bf16[384,2304]{1,0:T(8,128)(2,1)}, bf16[384,768]{1,0:T(8,128)(2,1)}, ...) | async-done | bytes 7077904 | tf_op jit(solution)/shard_map/psum | solution.py:264
  (322 shorter events, 208.8 us)
Async XLA Ops:
  7.2 56.1 %all-gather.14.cloned.1.call-start = ((), (), s32[]{:S(2)}) async-start(), calls=%async_computation.4 | async-start | bytes 5308416 | tf_op jit(solution)/shard_map/all_gather | solution.py:81
  10.7 112.6 %all-gather.16.cloned.1.call-start = ((), (), s32[]{:S(2)}) async-start(), calls=%async_computation.5 | async-start | bytes 1769472 | tf_op jit(solution)/shard_map/all_gather | solution.py:84
  11.7 141.4 %all-gather.18.cloned.1.call-start = ((), (), s32[]{:S(2)}) async-start(), calls=%async_computation.6 | async-start | bytes 7077888 | tf_op jit(solution)/shard_map/all_gather | solution.py:88
  15.9 36.0 %copy-start.54 = (s32[1024]{0:T(1024)S(1)}, s32[1024]{0:T(1024)}, u32[]{:S(2)}) copy-start(s32[1024]{0:T(1024)} %param.21) | copy-start | bytes 12292
  15.9 36.0 %copy-start.48 = (f32[1536]{0:T(1024)S(1)}, f32[1536]{0:T(1024)}, u32[]{:S(2)}) copy-start(f32[1536]{0:T(1024)} %param.33) | copy-start | bytes 18436
  16.0 201.8 %all-gather.20.cloned.1.call-start = ((), (), s32[]{:S(2)}) async-start(), calls=%async_computation.7 | async-start | bytes 7077888 | tf_op jit(solution)/shard_map/all_gather | solution.py:90
  20.0 345.4 %reduce-scatter.7.cloned.1.call-start = ((), (), s32[]{:S(2)}) async-start(), calls=%async_computation.9 | async-start | bytes 1769472 | tf_op jit(solution)/shard_map/reduce_scatter | solution.py:254
  25.6 127.4 %copy-start.50 = (f32[768]{0:T(1024)}, f32[768]{0:T(1024)S(1)}, u32[]{:S(2)}) copy-start(f32[768]{0:T(1024)S(1)} %reshape.249) | copy-start | bytes 9220
  30.0 224.0 %copy-start.42 = (f32[768]{0:T(1024)}, f32[768]{0:T(1024)S(1)}, u32[]{:S(2)}) copy-start(f32[768]{0:T(1024)S(1)} %reshape.248) | copy-start | bytes 9220
  47.5 15.8 %copy-start.52 = (f32[768]{0:T(1024)}, f32[768]{0:T(1024)S(1)}, u32[]{:S(2)}) copy-start(f32[768]{0:T(1024)S(1)} %reshape.244) | copy-start | bytes 9220
  51.9 11.4 %copy-start.32 = (f32[768]{0:T(1024)}, f32[768]{0:T(1024)S(1)}, u32[]{:S(2)}) copy-start(f32[768]{0:T(1024)S(1)} %reshape.243) | copy-start | bytes 9220
  58.3 11.4 %copy-start.4 = (bf16[1024,768]{0,1:T(8,128)(2,1)}, bf16[1024,768]{0,1:T(8,128)(2,1)S(1)}, u32[]{:S(2)}) copy-start(bf16[1024,768]{0,1:T(8,128)(2,1)S(1)} %copy.83) | copy-start | bytes 4718596
  58.6 11.1 %copy-start.30 = (f32[1024]{0:T(1024)}, f32[1024]{0:T(1024)S(1)}, u32[]{:S(2)}) copy-start(f32[1024]{0:T(1024)S(1)} %broadcast_multiply_fusion.1) | copy-start | bytes 12292
  59.0 10.7 %copy-start.40 = (f32[1024]{0:T(1024)}, f32[1024]{0:T(1024)S(1)}, u32[]{:S(2)}) copy-start(f32[1024]{0:T(1024)S(1)} %fusion.72) | copy-start | bytes 12292
  59.1 10.6 %copy-start.36 = (f32[1024]{0:T(1024)}, f32[1024]{0:T(1024)S(1)}, u32[]{:S(2)}) copy-start(f32[1024]{0:T(1024)S(1)} %fusion.76) | copy-start | bytes 12292
  127.1 126.9 %copy-start.7 = (f32[1024,768]{0,1:T(8,128)}, f32[1024,768]{0,1:T(8,128)S(1)}, u32[]{:S(2)}) copy-start(f32[1024,768]{0,1:T(8,128)S(1)} %get-tuple-element.284) | copy-start | bytes 9437188
  127.1 126.9 %copy-start.34 = (f32[1024]{0:T(1024)}, f32[1024]{0:T(1024)S(1)}, u32[]{:S(2)}) copy-start(f32[1024]{0:T(1024)S(1)} %broadcast_multiply_fusion) | copy-start | bytes 12292
  127.5 126.5 %copy-start.44 = (f32[1024]{0:T(1024)}, f32[1024]{0:T(1024)S(1)}, u32[]{:S(2)}) copy-start(f32[1024]{0:T(1024)S(1)} %fusion.77) | copy-start | bytes 12292
  259.9 124.9 %reduce-scatter.5.cloned.1.call-start = ((), (), s32[]{:S(2)}) async-start(), calls=%async_computation.8 | async-start | bytes 5308416 | tf_op jit(solution)/shard_map/reduce_scatter | solution.py:245
  336.9 110.2 %reduce-scatter.11.cloned.1.call-start = ((), (), s32[]{:S(2)}) async-start(), calls=%async_computation.11 | async-start | bytes 7077888 | tf_op jit(solution)/shard_map/reduce_scatter | solution.py:199
  346.2 164.0 %reduce-scatter.9.cloned.1.call-start = ((), (), s32[]{:S(2)}) async-start(), calls=%async_computation.10 | async-start | bytes 7077888 | tf_op jit(solution)/shard_map/reduce_scatter | solution.py:193
  356.8 309.4 %all-reduce.14.cloned.1.call-start = ((), (), s32[]{:S(2)}) async-start(), calls=%async_computation.12 | async-start | bytes 14155776 | tf_op jit(solution)/shard_map/psum | solution.py:264
  540.3 76.2 %copy-start.13 = (bf16[1024,768]{0,1:T(8,128)(2,1)S(1)}, bf16[1024,768]{0,1:T(8,128)(2,1)}, u32[]{:S(2)}) copy-start(bf16[1024,768]{0,1:T(8,128)(2,1)} %copy.92) | copy-start | bytes 4718596
  540.3 76.2 %copy-start.39 = (f32[1024]{0:T(1024)S(1)}, f32[1024]{0:T(1024)}, u32[]{:S(2)}) copy-start(f32[1024]{0:T(1024)} %copy-done.38) | copy-start | bytes 12292
  (56 other events, 170.8 us)
Sparse Core Ops, SparseCore 0:
  10.8 52.3 all-gather.13
  65.4 22.7 all-gather.15
  90.4 62.6 all-gather.17
  155.0 62.6 all-gather.19
  260.0 21.7 reduce-scatter.6
  337.1 47.6 reduce-scatter.4
  387.1 59.9 reduce-scatter.10
  450.1 59.9 reduce-scatter.8
  514.2 151.9 all-reduce.13
where the time goes:
time: 692 us; the launch traced here: 684 us
  waiting for transfers between devices  240 us (35%)
  matrix products  172 us (25%)
  blocking collectives  109 us (16%)
  local copies, waits for them, and re-layouts  75 us (11%)
  other arithmetic  69.7 us (10%)
  between operations  16.6 us (2%)
    reduce_scatter x1, waiting for transfers between devices, body(): lax.psum_scatter(grad_wup.astype(jnp.bfloat16), 'fsdp', scatter_dimension...  63 us
    reduce_scatter x1, waiting for transfers between devices, body(): lax.psum_scatter(grad_wdown.astype(jnp.bfloat16), 'fsdp', scatter_dimensi...  62.3 us
    psum x1, blocking collectives, body(): lax.psum(attn_shards[0].astype(jnp.bfloat16), 'dp').astype(jnp.float32)  61.8 us
    dot_general x4, matrix products, matmul(): return jnp.dot(left, right, preferred_element_type=jnp.float32)  57.9 us
    dot_general x4, matrix products, back_mul(): jnp.einsum('tb,ab->ta', left, right, preferred_element_type=jnp.float32)  41.1 us
    psum x1, waiting for transfers between devices, body(): lax.psum(attn_shards[2].astype(jnp.bfloat16), 'dp').astype(jnp.float32)  40.3 us
    dot_general x4, matrix products, outer_sum(): jnp.einsum('ta,tb->ab', left, right, preferred_element_type=jnp.float32)  27.2 us
    all_gather x1, waiting for transfers between devices, body(): lax.all_gather(rounded_params[11], 'fsdp', axis=0, tiled=True)  26.9 us
  transfers between devices with their start and end apart: 9, of which 7 were waited for; matrix products, arithmetic and copies ran while one was open for 37% of the time, Pallas kernels for 0%

commit v1 on v0

--- a/solution.py
+++ b/solution.py
@@ -258,8 +258,12 @@
             grad_obias.astype(jnp.bfloat16), "fsdp", scatter_dimension=0, tiled=True
         ).astype(jnp.float32),
     )
+
+    def refer_the_ports(x_part, axis_key):
+        return jnp.sum(lax.all_gather(x_part, axis_key), axis=0)
+
     attn_grads = (
-        lax.psum(attn_shards[0].astype(jnp.bfloat16), "dp").astype(jnp.float32),
+        refer_the_ports(attn_shards[0].astype(jnp.bfloat16), "dp").astype(jnp.float32),
         lax.psum(attn_shards[1].astype(jnp.bfloat16), "dp").astype(jnp.float32),
         lax.psum(attn_shards[2].astype(jnp.bfloat16), "dp").astype(jnp.float32),
         lax.psum(attn_shards[3].astype(jnp.bfloat16), "dp").astype(jnp.float32),

time: 692 us -> 692 us (level)
  blocking collectives: 109 us -> 127 us
  waiting for transfers between devices: 240 us -> 223 us
    all_gather x0 -> x1, blocking collectives: none -> 17.5 us  [refer_the_ports(): return jnp.sum(lax.all_gather(x_part, axis_key), axis=0)]
    psum x1, waiting for transfers between devices: 40.3 us -> 23 us  [body(): lax.psum(attn_shards[2].astype(jnp.bfloat16), 'dp').astype(jnp.float32)]
    unnamed x147 -> x148, local copies, waits for them, and re-layouts: 18.2 us -> 18.2 us
where the time goes in v1:
time: 692 us; the launch traced here: 684 us
  waiting for transfers between devices  223 us (32%)
  matrix products  172 us (25%)
  blocking collectives  127 us (18%)
  local copies, waits for them, and re-layouts  75 us (11%)
  other arithmetic  69.6 us (10%)
  between operations  16.6 us (2%)
    reduce_scatter x1, waiting for transfers between devices, body(): lax.psum_scatter(grad_wup.astype(jnp.bfloat16), 'fsdp', scatter_dimension...  63 us
    reduce_scatter x1, waiting for transfers between devices, body(): lax.psum_scatter(grad_wdown.astype(jnp.bfloat16), 'fsdp', scatter_dimensi...  62.3 us
    psum x1, blocking collectives, body(): lax.psum(attn_shards[1].astype(jnp.bfloat16), 'dp').astype(jnp.float32)  61.8 us
    dot_general x4, matrix products, matmul(): return jnp.dot(left, right, preferred_element_type=jnp.float32)  57.8 us
    dot_general x4, matrix products, back_mul(): jnp.einsum('tb,ab->ta', left, right, preferred_element_type=jnp.float32)  41.1 us
    dot_general x4, matrix products, outer_sum(): jnp.einsum('ta,tb->ab', left, right, preferred_element_type=jnp.float32)  27.2 us
    all_gather x1, waiting for transfers between devices, body(): lax.all_gather(rounded_params[11], 'fsdp', axis=0, tiled=True)  27 us
    all_gather x1, waiting for transfers between devices, body(): lax.all_gather(rounded_params[9], 'fsdp', axis=0, tiled=True)  25.5 us
  transfers between devices with their start and end apart: 9, of which 7 were waited for; matrix products, arithmetic and copies ran while one was open for 37% of the time, Pallas kernels for 0%

profile of v1, /device:TPU:0, one launch (start us, length us, event | category | flops | bytes accessed | tf_op | source)
XLA Modules:
  0.0 684.3 jit_solution(10078024031572251950)
XLA Ops:
  63.3 6.4 add_convert_fusion.1
  96.9 20.6 %while.26 = (s32[]{:T(128)}, bf16[2,512,12,64]{1,3,2,0:T(8,128)(2,1)}, f32[2,12,512,1]{2,1,3,0:T(8,128)S(1)}, bf16[2,512,12,64]{1,3,2,0:T(8,128)(2,1)}, s32[2,51...) while((s32[]{:T(128)}, ...), condition=%wide.region_5.6_spmd, body=%wide.region_2.5_spmd.sunk | while | flops 840558592 | bytes 42180708 | solution.py:156
  127.6 25.5 %all-gather.20.cloned.1.call-done = bf16[768,3072]{1,0:T(8,128)(2,1)} async-done(((bf16[384,3072]{1,0:T(8,128)(2,1)}), bf16[768,3072]{1,0:T(8,128)(2,1)}) %all-gather.20.cloned.1.call-update) | async-done | bytes 4718608 | tf_op jit(solution)/shard_map/all_gather | solution.py:88
  153.0 37.6 %multiply_convert_fusion.3 = (bf16[1024,3072]{1,0:T(8,128)(2,1)}, f32[1024,3072]{1,0:T(8,128)}, f32[1024,3072]{1,0:T(8,128)}) fusion(f32[3072]{0:T(1024)S(1)} %bitcast.168, bf16[768,3072]{1,0:T(8,128)(2,1)} %all-gather.20.cloned.1.call-done, f32[1024,768]{0,1:T(8,128)S(1)} %get-tuple-element.283, f32[768]{0:T(1024)S(1)} %reshape.252, ...), kind=kOutput, calls=%fused_computation.68 | convolution fusion | flops 5043388416 | bytes 39348224 | tf_op jit(solution)/shard_map/dot_general | solution.py:23
  190.7 27.0 %all-gather.22.cloned.1.call-done = bf16[3072,768]{1,0:T(8,128)(2,1)} async-done(((bf16[1536,768]{1,0:T(8,128)(2,1)}), bf16[3072,768]{1,0:T(8,128)(2,1)}) %all-gather.22.cloned.1.call-update) | async-done | bytes 4718608 | tf_op jit(solution)/shard_map/all_gather | solution.py:90
  217.7 18.9 %fusion.89 = (bf16[3072]{0:T(1024)(128)(2,1)}, bf16[1024,3072]{1,0:T(8,128)(2,1)}) fusion(f32[1024,3072]{1,0:T(8,128)} %get-tuple-element.274, bf16[1024,768]{1,0:T(8,128)(2,1)} %param.22, bf16[3072,768]{1,0:T(8,128)(2,1)} %all-gather.22.cloned.1.call-done, f32[1024,3072]{1,0:T(8,128)} %get-tuple-element.284, f32[3072]{0:T(1024)S(1)} %bitcast.169), kind=kOutput, calls=%fused_computation.142 | convolution fusion | flops 4882166784 | bytes 37767168 | tf_op jit(solution)/shard_map/tb,ab->ta/dot_general | solution.py:31
  236.6 10.3 %fusion.88 = (bf16[768]{0:T(1024)(128)(2,1)}, f32[1024,768]{1,0:T(8,128)}) fusion(bf16[1024,3072]{1,0:T(8,128)(2,1)} %get-tuple-element.290, bf16[768,3072]{1,0:T(8,128)(2,1)} %all-gather.20.cloned.1.call-done), kind=kOutput, calls=%fused_computation.141 | convolution fusion | flops 4832623616 | bytes 14157312 | tf_op jit(solution)/shard_map/tb,ab->ta/dot_general | solution.py:31
  270.5 49.0 %while.27 = (s32[]{:T(128)}, bf16[2,512,12,64]{1,3,2,0:T(8,128)(2,1)}, bf16[2,512,12,64]{1,3,2,0:T(8,128)(2,1)}, bf16[2,512,12,64]{1,3,2,0:T(8,128)(2,1)}, bf16[...) while((s32[]{:T(128)}, ...), condition=%wide.region_12.13_spmd, body=%wide.region_10.12_spmd.sunk | while | flops 2062673920 | bytes 141233456 | solution.py:225
  276.6 6.9 %multiply_reduce_fusion.5 = (f32[12,512]{1,0:T(8,128)S(1)}, f32[12,512,512]{1,2,0:T(8,128)}) fusion(f32[12,512,512]{1,2,0:T(8,128)S(1)} %fusion.138, f32[12,512]{1,0:T(8,128)S(1)} %dynamic-slice_bitcast_fusion.2, pred[512,512]{0,1:T(8,128)(4,1)S(1)} %broadcast_compare_fusion.5, bf16[2,512,12,64]{1,3,2,0:T(8,128)(2,1)S(1)} %copy-done.10, ...), kind=kOutput, calls=%fused_computation.25.clone.1 | convolution fusion | flops 418375680 | bytes 27059200 | tf_op jit(solution)/shard_map/while/body/eval_jaxpr/qhd,khd->hqk/dot_general | solution.py:127
  283.5 7.1 %multiply_convert_fusion.5 = bf16[12,512,512]{1,2,0:T(8,128)(2,1)S(1)} fusion(f32[12,512,512]{1,2,0:T(8,128)} %get-tuple-element.405, f32[12,512,512]{1,2,0:T(8,128)S(1)} %fusion.138, f32[12,512]{1,0:T(8,128)S(1)} %get-tuple-element.406, f32[12,512]{1,0:T(8,128)S(1)} %dynamic-slice_bitcast_fusion.2, pred[512,512]{0,1:T(8,128)(4,1)S(1)} %broadcast_compare_fusion.5), kind=kLoop, calls=%fused_computation.24.clone.1 | loop fusion | flops 18874368 | bytes 31768576 | tf_op jit(solution)/shard_map/while/body/eval_jaxpr/convert_element_type | solution.py:131
  301.0 6.9 %multiply_reduce_fusion.5 = (f32[12,512]{1,0:T(8,128)S(1)}, f32[12,512,512]{1,2,0:T(8,128)}) fusion(f32[12,512,512]{1,2,0:T(8,128)S(1)} %fusion.138, f32[12,512]{1,0:T(8,128)S(1)} %dynamic-slice_bitcast_fusion.2, pred[512,512]{0,1:T(8,128)(4,1)S(1)} %broadcast_compare_fusion.5, bf16[2,512,12,64]{1,3,2,0:T(8,128)(2,1)S(1)} %copy-done.10, ...), kind=kOutput, calls=%fused_computation.25.clone.1 | convolution fusion | flops 418375680 | bytes 27059200 | tf_op jit(solution)/shard_map/while/body/eval_jaxpr/qhd,khd->hqk/dot_general | solution.py:127
  307.9 7.1 %multiply_convert_fusion.5 = bf16[12,512,512]{1,2,0:T(8,128)(2,1)S(1)} fusion(f32[12,512,512]{1,2,0:T(8,128)} %get-tuple-element.405, f32[12,512,512]{1,2,0:T(8,128)S(1)} %fusion.138, f32[12,512]{1,0:T(8,128)S(1)} %get-tuple-element.406, f32[12,512]{1,0:T(8,128)S(1)} %dynamic-slice_bitcast_fusion.2, pred[512,512]{0,1:T(8,128)(4,1)S(1)} %broadcast_compare_fusion.5), kind=kLoop, calls=%fused_computation.24.clone.1 | loop fusion | flops 18874368 | bytes 31768576 | tf_op jit(solution)/shard_map/while/body/eval_jaxpr/convert_element_type | solution.py:131
  337.0 9.1 %convolution_convert_fusion = bf16[3072,768]{1,0:T(8,128)(2,1)} fusion(bf16[1024,3072]{1,0:T(8,128)(2,1)} %get-tuple-element.273, bf16[1024,768]{1,0:T(8,128)(2,1)} %param.22), kind=kOutput, calls=%fused_computation.83 | convolution fusion | flops 4834197504 | bytes 12582912 | tf_op jit(solution)/shard_map/ta,tb->ab/dot_general | solution.py:27
  346.8 10.0 %convolution_convert_fusion.1 = bf16[768,3072]{1,0:T(8,128)(2,1)} fusion(bf16[1024,3072]{1,0:T(8,128)(2,1)} %get-tuple-element.290, f32[1024,768]{0,1:T(8,128)} %copy-done.7, f32[768]{0:T(1024)S(1)} %copy-done.51, f32[768]{0:T(1024)S(1)} %copy-done.43, f32[1024]{0:T(1024)S(1)} %copy-done.45, f32[1024]{0:T(1024)S(1)} %copy-done.35), kind=kOutput, calls=%fused_computation.84 | convolution fusion | flops 4838129664 | bytes 14170112 | tf_op jit(solution)/shard_map/ta,tb->ab/dot_general | solution.py:27
  365.4 19.4 %reduce-scatter.5.cloned.1.call-done = bf16[384,2304]{1,0:T(8,128)(2,1)} async-done(((bf16[768,2304]{1,0:T(8,128)(2,1)}), bf16[384,2304]{1,0:T(8,128)(2,1)}) %reduce-scatter.5.cloned.1.call-update) | async-done | bytes 1769488 | tf_op jit(solution)/shard_map/reduce_scatter | solution.py:245
  384.8 62.3 %reduce-scatter.11.cloned.1.call-done = bf16[1536,768]{1,0:T(8,128)(2,1)} async-done(((bf16[3072,768]{1,0:T(8,128)(2,1)}), bf16[1536,768]{1,0:T(8,128)(2,1)}) %reduce-scatter.11.cloned.1.call-update) | async-done | bytes 2359312 | tf_op jit(solution)/shard_map/reduce_scatter | solution.py:199
  447.1 63.0 %reduce-scatter.9.cloned.1.call-done = bf16[384,3072]{1,0:T(8,128)(2,1)} async-done(((bf16[768,3072]{1,0:T(8,128)(2,1)}), bf16[384,3072]{1,0:T(8,128)(2,1)}) %reduce-scatter.9.cloned.1.call-update) | async-done | bytes 2359312 | tf_op jit(solution)/shard_map/reduce_scatter | solution.py:193
  510.2 10.0 %add_convert_fusion.3 = bf16[1024,768]{0,1:T(8,128)(2,1)} fusion(f32[1024,768]{0,1:T(8,128)} %copy-done.7, bf16[1024,3072]{1,0:T(8,128)(2,1)} %get-tuple-element.273, bf16[3072,768]{1,0:T(8,128)(2,1)} %all-gather.22.cloned.1.call-done, f32[768]{0:T(1024)S(1)} %reshape.254), kind=kOutput, calls=%fused_computation.106 | convolution fusion | flops 4834197504 | bytes 15731712 | tf_op jit(solution)/shard_map/dot_general | solution.py:23
  524.9 9.1 %fusion.87 = (bf16[768]{0:T(1024)(128)(2,1)S(1)}, f32[1024,768]{1,0:T(8,128)}) fusion(bf16[1024,2304]{0,1:T(8,128)(2,1)} %copy-done.25, bf16[768,2304]{1,0:T(8,128)(2,1)} %all-gather.16.cloned.1.call-done), kind=kOutput, calls=%fused_computation.140 | convolution fusion | flops 3624664320 | bytes 11404800 | tf_op jit(solution)/shard_map/tb,ab->ta/dot_general | solution.py:31
  541.9 7.4 %all-reduce.11 = (bf16[768]{0:T(1024)(128)(2,1)S(1)}, bf16[768]{0:T(1024)(128)(2,1)S(1)}, bf16[768]{0:T(1024)(128)(2,1)S(1)}, bf16[768]{0:T(1024)(128)(2,1)S(1)}...) all-reduce(bf16[768]{0:T(1024)(128)(2,1)S(1)} %get-tuple-element.21, ...), channel_id=3, replica_groups=mesh['dp'=16,'fsdp'=2] {'fsdp'}, use_global_device_ids=true, to_apply=%region_16.17.clone | all-reduce | flops 9216 | bytes 36864
  550.0 61.8 %all-reduce.9 = (bf16[384]{0:T(512)(128)(2,1)S(1)}, bf16[384]{0:T(512)(128)(2,1)S(1)}, bf16[384]{0:T(512)(128)(2,1)S(1)}, bf16[384]{0:T(512)(128)(2,1)S(1)}, bf1...) all-reduce(bf16[384]{0:T(512)(128)(2,1)S(1)} %dynamic-slice.3, ...), channel_id=1, replica_groups=mesh['dp'=16,'fsdp'=2] {'dp'}, use_global_device_ids=true, to_apply=%region_20.21 | all-reduce | flops 4224 | bytes 16896 | tf_op jit(solution)/shard_map/psum | solution.py:267
  615.9 6.0 add_convert_fusion.2
  625.1 17.5 %all-gather.10 = bf16[16,1,384]{2,1,0:T(2,128)(2,1)S(1)} all-gather(bf16[1,1,384]{2,1,0:T(2,128)(2,1)S(1)} %reshape.244), channel_id=2, replica_groups=mesh['dp'=16,'fsdp'=2] {'dp'}, dimensions={0}, use_global_device_ids=true | all-gather | bytes 13056 | tf_op jit(solution)/shard_map/all_gather | solution.py:263
  643.2 23.0 %all-reduce.14.cloned.1.call-done = (bf16[384,2304]{1,0:T(8,128)(2,1)}, bf16[384,768]{1,0:T(8,128)(2,1)}, bf16[384,3072]{1,0:T(8,128)(2,1)}, bf16[1536,768]{1,0:T(8,128)(2,1)}) async-done(((bf16[384,2304]{1,0:T(8,128)(2,1)}, bf16[384,768]{1,0:T(8,128)(2,1)}, bf16[384,3072]{1,0:T(8,128)(2,1)}, bf16[1536,768]{1,0:T(8,128)(2,1)}), (bf16[384,2304]{1,0:T(8,128)(2,1)}, bf16[384,768]{1,0:T(8,128)(2,1)}, ...) | async-done | bytes 7077904 | tf_op jit(solution)/shard_map/psum | solution.py:268
  (325 shorter events, 214.5 us)
Async XLA Ops:
  7.2 56.1 %all-gather.16.cloned.1.call-start = ((), (), s32[]{:S(2)}) async-start(), calls=%async_computation.4 | async-start | bytes 5308416 | tf_op jit(solution)/shard_map/all_gather | solution.py:81
  10.7 112.6 %all-gather.18.cloned.1.call-start = ((), (), s32[]{:S(2)}) async-start(), calls=%async_computation.5 | async-start | bytes 1769472 | tf_op jit(solution)/shard_map/all_gather | solution.py:84
  11.7 141.4 %all-gather.20.cloned.1.call-start = ((), (), s32[]{:S(2)}) async-start(), calls=%async_computation.6 | async-start | bytes 7077888 | tf_op jit(solution)/shard_map/all_gather | solution.py:88
  15.9 36.0 %copy-start.54 = (s32[1024]{0:T(1024)S(1)}, s32[1024]{0:T(1024)}, u32[]{:S(2)}) copy-start(s32[1024]{0:T(1024)} %param.21) | copy-start | bytes 12292
  15.9 36.0 %copy-start.48 = (f32[1536]{0:T(1024)S(1)}, f32[1536]{0:T(1024)}, u32[]{:S(2)}) copy-start(f32[1536]{0:T(1024)} %param.33) | copy-start | bytes 18436
  16.0 201.8 %all-gather.22.cloned.1.call-start = ((), (), s32[]{:S(2)}) async-start(), calls=%async_computation.7 | async-start | bytes 7077888 | tf_op jit(solution)/shard_map/all_gather | solution.py:90
  20.0 345.4 %reduce-scatter.7.cloned.1.call-start = ((), (), s32[]{:S(2)}) async-start(), calls=%async_computation.9 | async-start | bytes 1769472 | tf_op jit(solution)/shard_map/reduce_scatter | solution.py:254
  25.6 127.4 %copy-start.50 = (f32[768]{0:T(1024)}, f32[768]{0:T(1024)S(1)}, u32[]{:S(2)}) copy-start(f32[768]{0:T(1024)S(1)} %reshape.252) | copy-start | bytes 9220
  30.0 224.0 %copy-start.42 = (f32[768]{0:T(1024)}, f32[768]{0:T(1024)S(1)}, u32[]{:S(2)}) copy-start(f32[768]{0:T(1024)S(1)} %reshape.251) | copy-start | bytes 9220
  47.5 15.8 %copy-start.52 = (f32[768]{0:T(1024)}, f32[768]{0:T(1024)S(1)}, u32[]{:S(2)}) copy-start(f32[768]{0:T(1024)S(1)} %reshape.247) | copy-start | bytes 9220
  51.9 11.4 %copy-start.32 = (f32[768]{0:T(1024)}, f32[768]{0:T(1024)S(1)}, u32[]{:S(2)}) copy-start(f32[768]{0:T(1024)S(1)} %reshape.246) | copy-start | bytes 9220
  58.3 11.4 %copy-start.4 = (bf16[1024,768]{0,1:T(8,128)(2,1)}, bf16[1024,768]{0,1:T(8,128)(2,1)S(1)}, u32[]{:S(2)}) copy-start(bf16[1024,768]{0,1:T(8,128)(2,1)S(1)} %copy.83) | copy-start | bytes 4718596
  58.6 11.1 %copy-start.30 = (f32[1024]{0:T(1024)}, f32[1024]{0:T(1024)S(1)}, u32[]{:S(2)}) copy-start(f32[1024]{0:T(1024)S(1)} %broadcast_multiply_fusion.1) | copy-start | bytes 12292
  59.0 10.7 %copy-start.40 = (f32[1024]{0:T(1024)}, f32[1024]{0:T(1024)S(1)}, u32[]{:S(2)}) copy-start(f32[1024]{0:T(1024)S(1)} %fusion.72) | copy-start | bytes 12292
  59.1 10.6 %copy-start.36 = (f32[1024]{0:T(1024)}, f32[1024]{0:T(1024)S(1)}, u32[]{:S(2)}) copy-start(f32[1024]{0:T(1024)S(1)} %fusion.76) | copy-start | bytes 12292
  127.1 126.9 %copy-start.7 = (f32[1024,768]{0,1:T(8,128)}, f32[1024,768]{0,1:T(8,128)S(1)}, u32[]{:S(2)}) copy-start(f32[1024,768]{0,1:T(8,128)S(1)} %get-tuple-element.283) | copy-start | bytes 9437188
  127.2 126.9 %copy-start.34 = (f32[1024]{0:T(1024)}, f32[1024]{0:T(1024)S(1)}, u32[]{:S(2)}) copy-start(f32[1024]{0:T(1024)S(1)} %broadcast_multiply_fusion) | copy-start | bytes 12292
  127.6 126.5 %copy-start.44 = (f32[1024]{0:T(1024)}, f32[1024]{0:T(1024)S(1)}, u32[]{:S(2)}) copy-start(f32[1024]{0:T(1024)S(1)} %fusion.77) | copy-start | bytes 12292
  259.9 124.9 %reduce-scatter.5.cloned.1.call-start = ((), (), s32[]{:S(2)}) async-start(), calls=%async_computation.8 | async-start | bytes 5308416 | tf_op jit(solution)/shard_map/reduce_scatter | solution.py:245
  336.9 110.2 %reduce-scatter.11.cloned.1.call-start = ((), (), s32[]{:S(2)}) async-start(), calls=%async_computation.11 | async-start | bytes 7077888 | tf_op jit(solution)/shard_map/reduce_scatter | solution.py:199
  346.2 164.0 %reduce-scatter.9.cloned.1.call-start = ((), (), s32[]{:S(2)}) async-start(), calls=%async_computation.10 | async-start | bytes 7077888 | tf_op jit(solution)/shard_map/reduce_scatter | solution.py:193
  356.8 309.4 %all-reduce.14.cloned.1.call-start = ((), (), s32[]{:S(2)}) async-start(), calls=%async_computation.12 | async-start | bytes 14155776 | tf_op jit(solution)/shard_map/psum | solution.py:268
  540.3 75.6 %copy-start.13 = (bf16[1024,768]{0,1:T(8,128)(2,1)S(1)}, bf16[1024,768]{0,1:T(8,128)(2,1)}, u32[]{:S(2)}) copy-start(bf16[1024,768]{0,1:T(8,128)(2,1)} %copy.92) | copy-start | bytes 4718596
  540.3 75.6 %copy-start.39 = (f32[1024]{0:T(1024)S(1)}, f32[1024]{0:T(1024)}, u32[]{:S(2)}) copy-start(f32[1024]{0:T(1024)} %copy-done.38) | copy-start | bytes 12292
  (56 other events, 170.8 us)
Sparse Core Ops, SparseCore 0:
  10.8 52.3 all-gather.15
  65.4 22.7 all-gather.17
  90.4 62.6 all-gather.19
  155.0 62.6 all-gather.21
  260.0 21.7 reduce-scatter.6
  337.0 47.6 reduce-scatter.4
  387.1 59.9 reduce-scatter.10
  450.1 59.9 reduce-scatter.8
  514.2 152.0 all-reduce.13
